TPU v7x, 256 devices: a whole 4x4x8 slice. The times are simulated.
256 devices in a mesh: row: 16 (over z, y_lo), col: 16 (over y_hi, x, core).
Axes of the slice: x: 4, y: 4 (y_hi: 2, y_lo: 2; y = y_hi * 2 + y_lo), z: 8, core: 2. Of those that a mesh axis runs over, the one named last changes fastest.
Arguments:
- ancestor: float32 [8192, 8192], P('row', 'col'), may hold values from -0.0625 to 0.0625
- factor: float32 [8192, 16, 128], P(('row', 'col')), may hold values from -1.5 to 1.5
- diag_inv: float32 [16, 128, 128], replicated, may hold values from -6 to 6
- structure: int32 [16, 768], replicated, may hold values from 0 to 1023, as said below
Outputs:
- inverse_panel: float32 [8192, 16, 128], P(('row', 'col'))
- inverse_diagonal: float32 [16, 128, 128], replicated
Inputs may be any that keep to these rules, and one draw needn't show every extreme that they name: Each row of structure lists 768 different block numbers, in no particular order.
All inputs are finite; a program needn't handle non-finite values.
Results may differ from a plain program's by a relative error of at most 0.00007.
Values sent between devices are 32-bit elements; how exact they have to be, the bound alone decides.
No kernel may reach another device: no remote copies, remote signals or barrier semaphores. Data moves between devices by JAX's collectives and lax.ppermute only.
A program may use at most 64 MiB of HBM per device.

v0:
```python
import jax
import jax.numpy as jnp
from jax import lax
from jax.sharding import PartitionSpec as P

RB = 8


def spread_2(value, axis, source):
    kept = jnp.where(lax.axis_index(axis) == source, value, 0).astype(value.dtype)
    return lax.psum(kept, axis)


def per_device(ancestor, factor, diag_inv, structure):
    row_devices = lax.axis_size("row")
    col_devices = lax.axis_size("col")
    ratio = row_devices // col_devices
    local_rows = factor.shape[0]
    width = factor.shape[2]
    first_row = (lax.axis_index("row") * col_devices + lax.axis_index("col")) * local_rows
    block_ids = (first_row + jnp.arange(local_rows, dtype=jnp.int32)) // RB
    matches = block_ids[:, None, None] == structure[None, :, :]
    row_mask = jnp.any(matches, axis=2).astype(jnp.float32)
    masked = factor * row_mask[:, :, None]
    count_sib = masked.shape[1]
    spread = masked.reshape(local_rows, count_sib * width)
    block_row = lax.all_gather(spread, "col", axis=0, tiled=True)
    received = spread_2(block_row, "row", lax.axis_index("col") * ratio + 0)
    summed = lax.psum_scatter(
        jnp.dot(
            ancestor, received, precision=lax.Precision.HIGHEST, preferred_element_type=jnp.float32
        ),
        "col",
        scatter_dimension=0,
        tiled=True,
    )
    panel = -summed.reshape(local_rows, count_sib, width)
    panel = panel * row_mask[:, :, None]
    local_update = jnp.einsum("bsw,bsv->swv", masked, panel, precision=lax.Precision.HIGHEST)
    total_update = lax.psum(local_update, ("row", "col"))
    return (panel, diag_inv - total_update)


def solution(mesh):
    placed = (P("row", "col"), P(("row", "col"), None, None), P(), P())
    return jax.shard_map(
        per_device,
        mesh=mesh,
        in_specs=placed,
        out_specs=(P(("row", "col"), None, None), P()),
        check_vma=False,
    )
```

profile of v0, /device:TPU:2, one launch (start us, length us, event | category | flops | bytes accessed | tf_op | source)
XLA Modules:
  0.0 657.8 jit_solution(703054387542532473)
XLA Ops:
  7.2 0.0 copy-start
  7.2 0.0 all-gather.2.cloned.1.call-start
  7.2 1.6 compare_reduce_fusion
  8.8 1.1 broadcast_multiply_fusion.1
  9.9 0.8 copy.23
  10.7 0.0 all-gather.2.cloned.1.call-update
  10.7 0.0 all-reduce.3.cloned.1.call-start
  10.8 64.4 %all-gather.2.cloned.1.call-done = f32[512,2048]{1,0:T(8,128)} async-done(((f32[32,2048]{1,0:T(8,128)}), f32[512,2048]{1,0:T(8,128)}) %all-gather.2.cloned.1.call-update) | async-done | bytes 4194320 | tf_op jit(solution)/shard_map/all_gather | solution.py:27
  75.2 2.5 broadcast_select_fusion
  77.7 0.0 all-reduce.3.cloned.1.call-update
  77.7 0.0 reduce-scatter.4.cloned.1.call-start
  77.8 199.0 %all-reduce.3.cloned.1.call-done = f32[512,2048]{1,0:T(8,128)} async-done(((f32[512,2048]{1,0:T(8,128)}), f32[512,2048]{1,0:T(8,128)}) %all-reduce.3.cloned.1.call-update) | async-done | bytes 4194320 | tf_op jit(solution)/shard_map/psum | solution.py:11
  276.8 0.0 copy-done
  276.8 16.3 %convolution_bitcast_fusion = f32[512,2048]{0,1:T(8,128)} fusion(f32[512,2048]{1,0:T(8,128)} %all-reduce.3.cloned.1.call-done, f32[512,512]{1,0:T(8,128)S(1)} %copy-done), kind=kOutput, calls=%fused_computation | convolution fusion | flops 6442450944 | bytes 9437184 | tf_op jit(solution)/shard_map/dot_general | solution.py:30
  293.0 5.4 copy.15
  298.4 0.0 reduce-scatter.4.cloned.1.call-update
  298.5 0.0 all-reduce.5.cloned.1.call-start
  298.5 88.3 %reduce-scatter.4.cloned.1.call-done = f32[32,2048]{1,0:T(8,128)} async-done(((f32[512,2048]{1,0:T(8,128)}), f32[32,2048]{1,0:T(8,128)}) %reduce-scatter.4.cloned.1.call-update) | async-done | bytes 262160
  386.8 1.3 copy.16
  388.1 0.1 neg.6
  388.2 0.3 copy.12
  388.5 0.1 broadcast_multiply_fusion
  388.7 0.0 copy-start.1
  388.7 2.8 fusion
  391.5 0.0 all-reduce.5.cloned.1.call-update
  391.5 257.1 %all-reduce.5.cloned.1.call-done = f32[16,128,128]{2,1,0:T(8,128)} async-done(((f32[16,128,128]{2,1,0:T(8,128)}), f32[16,128,128]{2,1,0:T(8,128)}) %all-reduce.5.cloned.1.call-update) | async-done | bytes 1048592 | tf_op jit(solution)/shard_map/psum | solution.py:40
  648.6 2.6 sub.10
  651.3 0.0 copy-done.1
  (2 shorter events, 0.0 us)
Async XLA Ops:
  7.2 269.6 %copy-start = (f32[512,512]{1,0:T(8,128)S(1)}, f32[512,512]{1,0:T(8,128)}, u32[]{:S(2)}) copy-start(f32[512,512]{1,0:T(8,128)} %param.4) | copy-start | bytes 3145732
  7.2 68.0 %all-gather.2.cloned.1.call-start = ((), (), s32[]{:S(2)}) async-start(), calls=%async_computation.1 | async-start | bytes 4456448 | tf_op jit(solution)/shard_map/all_gather | solution.py:27
  10.7 266.0 %all-reduce.3.cloned.1.call-start = ((), (), s32[]{:S(2)}) async-start(), calls=%async_computation.2 | async-start | bytes 8388608 | tf_op jit(solution)/shard_map/psum | solution.py:11
  77.7 309.1 %reduce-scatter.4.cloned.1.call-start = ((), (), s32[]{:S(2)}) async-start(), calls=%async_computation.4 | async-start | bytes 4456448
  298.5 350.2 %all-reduce.5.cloned.1.call-start = ((), (), s32[]{:S(2)}) async-start(), calls=%async_computation.3 | async-start | bytes 2097152 | tf_op jit(solution)/shard_map/psum | solution.py:40
  388.7 262.6 %copy-start.1 = (f32[32,16,128]{2,1,0:T(8,128)}, f32[32,16,128]{2,1,0:T(8,128)S(1)}, u32[]{:S(2)}) copy-start(f32[32,16,128]{2,1,0:T(8,128)S(1)} %broadcast_multiply_fusion) | copy-start | bytes 786436
Sparse Core Ops, SparseCore 0:
  11.3 63.8 all-gather.1
  77.8 198.8 all-reduce.2
  298.6 88.2 reduce-scatter.3
  393.6 254.9 all-reduce.4
where the time goes:
time: 658 us
  waiting for transfers between devices  609 us (93%)
  matrix products  19.1 us (3%)
  between operations  13.8 us (2%)
  other arithmetic  8.03 us (1%)
  local copies, waits for them, and re-layouts  7.8 us (1%)
    psum x1, waiting for transfers between devices, per_device(): total_update = lax.psum(local_update, ('row', 'col'))  257 us
    psum x1, waiting for transfers between devices, spread_2(): return lax.psum(kept, axis)  199 us
    unnamed x5, waiting for transfers between devices  88.4 us
    all_gather x1, waiting for transfers between devices, per_device(): block_row = lax.all_gather(spread, 'col', axis=0, tiled=True)  64.4 us
    dot_general x1, matrix products, per_device(): jnp.dot(ancestor, received, precision=lax.Precision.HIGHEST, preferred_el...  16.3 us
  transfers between devices with their start and end apart: 4, of which 4 were waited for; matrix products, arithmetic and copies ran while one was open for 0% of the time, Pallas kernels for 0%

commit v1 on v0

--- a/solution.py
+++ b/solution.py
@@ -1,9 +1,18 @@
+import functools
 import jax
 import jax.numpy as jnp
 from jax import lax
 from jax.sharding import PartitionSpec as P
 
 RB = 8
+
+
+def _step_on_entries(mine, axis_key, ax_name):
+    val2 = lax.psum(mine, axis_name=axis_key)
+    return lax.psum(val2, axis_name=ax_name)
+
+
+point_the_pieces_all = functools.partial(_step_on_entries, axis_key="row", ax_name="col")
 
 
 def spread_2(value, axis, source):
@@ -37,7 +46,7 @@
     panel = -summed.reshape(local_rows, count_sib, width)
     panel = panel * row_mask[:, :, None]
     local_update = jnp.einsum("bsw,bsv->swv", masked, panel, precision=lax.Precision.HIGHEST)
-    total_update = lax.psum(local_update, ("row", "col"))
+    total_update = point_the_pieces_all(local_update)
     return (panel, diag_inv - total_update)
 
 

time: 658 us -> 688 us (1.046)
  waiting for transfers between devices: 609 us -> 634 us
    psum x1 -> x2, waiting for transfers between devices: 257 us -> 282 us  [the longest x1 143 us: _step_on_entries(): return lax.psum(val2, axis_name=ax_name)]
    unnamed x5 -> x6, waiting for transfers between devices: 88.4 us -> 88.4 us
  transfers between devices with their start and end apart: 4 -> 5, of which waited for: 4 -> 5; matrix products, arithmetic and copies ran while one was open for 0% -> 0% of each run, Pallas kernels for 0% -> 0%
where the time goes in v1:
time: 688 us; the launch traced here: 683 us
  waiting for transfers between devices  634 us (92%)
  matrix products  19.1 us (3%)
  between operations  13.9 us (2%)
  other arithmetic  8.03 us (1%)
  local copies, waits for them, and re-layouts  7.8 us (1%)
    psum x1, waiting for transfers between devices, spread_2(): return lax.psum(kept, axis)  199 us
    psum x1, waiting for transfers between devices, _step_on_entries(): return lax.psum(val2, axis_name=ax_name)  143 us
    psum x1, waiting for transfers between devices, _step_on_entries(): val2 = lax.psum(mine, axis_name=axis_key)  139 us
    unnamed x6, waiting for transfers between devices  88.4 us
    all_gather x1, waiting for transfers between devices, per_device(): block_row = lax.all_gather(spread, 'col', axis=0, tiled=True)  64.4 us
    dot_general x1, matrix products, per_device(): jnp.dot(ancestor, received, precision=lax.Precision.HIGHEST, preferred_el...  16.3 us
  transfers between devices with their start and end apart: 5, of which 5 were waited for; matrix products, arithmetic and copies ran while one was open for 0% of the time, Pallas kernels for 0%

profile of v1, /device:TPU:2, one launch (start us, length us, event | category | flops | bytes accessed | tf_op | source)
XLA Modules:
  0.0 682.5 jit_solution(16789772689252889416)
XLA Ops:
  7.2 0.0 copy-start
  7.2 0.0 all-gather.2.cloned.1.call-start
  7.2 1.6 compare_reduce_fusion
  8.8 1.1 broadcast_multiply_fusion.1
  9.9 0.8 copy.23
  10.7 0.0 all-gather.2.cloned.1.call-update
  10.7 0.0 all-reduce.4.cloned.1.call-start
  10.8 64.4 %all-gather.2.cloned.1.call-done = f32[512,2048]{1,0:T(8,128)} async-done(((f32[32,2048]{1,0:T(8,128)}), f32[512,2048]{1,0:T(8,128)}) %all-gather.2.cloned.1.call-update) | async-done | bytes 4194320 | tf_op jit(solution)/shard_map/all_gather | solution.py:36
  75.2 2.5 broadcast_select_fusion
  77.7 0.0 all-reduce.4.cloned.1.call-update
  77.7 0.0 reduce-scatter.4.cloned.1.call-start
  77.8 199.0 %all-reduce.4.cloned.1.call-done = f32[512,2048]{1,0:T(8,128)} async-done(((f32[512,2048]{1,0:T(8,128)}), f32[512,2048]{1,0:T(8,128)}) %all-reduce.4.cloned.1.call-update) | async-done | bytes 4194320 | tf_op jit(solution)/shard_map/psum | solution.py:20
  276.8 0.0 copy-done
  276.8 16.3 %convolution_bitcast_fusion = f32[512,2048]{0,1:T(8,128)} fusion(f32[512,2048]{1,0:T(8,128)} %all-reduce.4.cloned.1.call-done, f32[512,512]{1,0:T(8,128)S(1)} %copy-done), kind=kOutput, calls=%fused_computation | convolution fusion | flops 6442450944 | bytes 9437184 | tf_op jit(solution)/shard_map/dot_general | solution.py:39
  293.0 5.4 copy.15
  298.4 0.0 reduce-scatter.4.cloned.1.call-update
  298.5 0.0 all-reduce.6.cloned.1.call-start
  298.5 88.3 %reduce-scatter.4.cloned.1.call-done = f32[32,2048]{1,0:T(8,128)} async-done(((f32[512,2048]{1,0:T(8,128)}), f32[32,2048]{1,0:T(8,128)}) %reduce-scatter.4.cloned.1.call-update) | async-done | bytes 262160
  386.8 1.3 copy.16
  388.1 0.1 neg.6
  388.2 0.3 copy.12
  388.5 0.1 broadcast_multiply_fusion
  388.7 0.0 copy-start.1
  388.7 2.8 fusion
  391.5 0.0 all-reduce.6.cloned.1.call-update
  391.5 0.0 all-reduce.8.cloned.1.call-start
  391.6 138.6 %all-reduce.6.cloned.1.call-done = f32[16,128,128]{2,1,0:T(8,128)} async-done(((f32[16,128,128]{2,1,0:T(8,128)}), f32[16,128,128]{2,1,0:T(8,128)}) %all-reduce.6.cloned.1.call-update) | async-done | bytes 1048592 | tf_op jit(solution)/shard_map/psum | solution.py:11
  530.1 0.0 all-reduce.8.cloned.1.call-update
  530.1 143.2 %all-reduce.8.cloned.1.call-done = f32[16,128,128]{2,1,0:T(8,128)} async-done(((f32[16,128,128]{2,1,0:T(8,128)}), f32[16,128,128]{2,1,0:T(8,128)}) %all-reduce.8.cloned.1.call-update) | async-done | bytes 1048592 | tf_op jit(solution)/shard_map/psum | solution.py:12
  673.3 2.6 sub.10
  676.0 0.0 copy-done.1
  (2 shorter events, 0.0 us)
Async XLA Ops:
  7.2 269.6 %copy-start = (f32[512,512]{1,0:T(8,128)S(1)}, f32[512,512]{1,0:T(8,128)}, u32[]{:S(2)}) copy-start(f32[512,512]{1,0:T(8,128)} %param.4) | copy-start | bytes 3145732
  7.2 68.0 %all-gather.2.cloned.1.call-start = ((), (), s32[]{:S(2)}) async-start(), calls=%async_computation.1 | async-start | bytes 4456448 | tf_op jit(solution)/shard_map/all_gather | solution.py:36
  10.7 266.0 %all-reduce.4.cloned.1.call-start = ((), (), s32[]{:S(2)}) async-start(), calls=%async_computation.2 | async-start | bytes 8388608 | tf_op jit(solution)/shard_map/psum | solution.py:20
  77.7 309.1 %reduce-scatter.4.cloned.1.call-start = ((), (), s32[]{:S(2)}) async-start(), calls=%async_computation.5 | async-start | bytes 4456448
  298.5 231.7 %all-reduce.6.cloned.1.call-start = ((), (), s32[]{:S(2)}) async-start(), calls=%async_computation.3 | async-start | bytes 2097152 | tf_op jit(solution)/shard_map/psum | solution.py:11
  388.7 287.3 %copy-start.1 = (f32[32,16,128]{2,1,0:T(8,128)}, f32[32,16,128]{2,1,0:T(8,128)S(1)}, u32[]{:S(2)}) copy-start(f32[32,16,128]{2,1,0:T(8,128)S(1)} %broadcast_multiply_fusion) | copy-start | bytes 786436
  391.5 281.8 %all-reduce.8.cloned.1.call-start = ((), (), s32[]{:S(2)}) async-start(), calls=%async_computation.4 | async-start | bytes 2097152 | tf_op jit(solution)/shard_map/psum | solution.py:12
Sparse Core Ops, SparseCore 0:
  11.3 63.8 all-gather.1
  77.8 198.8 all-reduce.3
  298.6 88.2 reduce-scatter.3
  391.6 138.4 all-reduce.5
  532.6 140.6 all-reduce.7
